TPU v7x, 512 devices: a whole 4x8x8 slice. The times are simulated.
512 devices in a mesh: sub: 64 (over y, z), crow: 4 (over x_lo, core), ccol: 2 (over x_hi).
Axes of the slice: x: 4 (x_hi: 2, x_lo: 2; x = x_hi * 2 + x_lo), y: 8, z: 8, core: 2. Of those that a mesh axis runs over, the one named last changes fastest.
Arguments:
- loads: bfloat16 [128, 1024, 128], P('sub'), may hold values from -6 to 6
- stiffness: bfloat16 [128, 1024, 1024], P('sub', ('crow', 'ccol'))
- local_inverse: bfloat16 [128, 1024, 1024], P('sub', ('crow', 'ccol'))
- coarse_basis: bfloat16 [128, 1024, 48], P('sub', ('crow', 'ccol')), may hold values from -0.1875 to 0.1875
- coarse_inverse: bfloat16 [6144, 6144], P('sub', ('crow', 'ccol'))
- coarse_index: int32 [128, 48], P('sub'), may hold values from 0 to 6143, as said below
- left_rows: int32 [128, 128], P('sub'), may hold values from 0 to 1023, as said below
- right_rows: int32 [128, 128], P('sub'), may hold values from 0 to 1023, as said below
Outputs:
- second_pass: float32 [128, 1024, 128], P('sub', ('crow', 'ccol'))
- final_residual: float32 [128, 1024, 128], P('sub', ('crow', 'ccol'))
Inputs may be any that keep to these rules, and one draw needn't show every extreme that they name: `coarse_index`: every value 0 to 6143 appears exactly once in the whole array. Of the 96 values in the rows of one index of sub, at most 24 lie in one block of 768 consecutive coarse rows starting at a multiple of 768, and that most is reached. In each subdomain the 128 entries of left_rows and the 128 entries of right_rows are 256 distinct rows. `right_rows`: see left_rows.
All inputs are finite; a program needn't handle non-finite values.
Results may differ from a plain program's by a relative error of at most 0.0067.
Values may be sent and summed in bfloat16 or wider, within the bound.
A program may use at most 64 MiB of HBM per device.

v0:
```python
import jax
import jax.numpy as jnp
from jax import lax
from jax.sharding import PartitionSpec as P


def padded(block, sides, width):
    for axis, dim in sides:
        count = lax.axis_size(axis)
        forward = [(i, i + 1) for i in range(count - 1)]
        forward.append((count - 1, 0))
        backward = [(target, source) for source, target in forward]
        low = lax.ppermute(
            lax.slice_in_dim(block, block.shape[dim] - width, None, axis=dim), axis, forward
        )
        high = lax.ppermute(lax.slice_in_dim(block, 0, width, axis=dim), axis, backward)
        block = jnp.concatenate([low, block, high], axis=dim)
    return block


def fold_product(matrix, gathered_piece):
    return jnp.einsum("sij,sjc->sic", matrix, gathered_piece, preferred_element_type=jnp.float32)


def apply_stiffness(iterate, stiffness, pick_left, pick_right):
    sub_count, row_count, case_count = iterate.shape
    rounded = iterate.astype(jnp.bfloat16)
    product = fold_product(stiffness, lax.all_gather(rounded, ("crow", "ccol"), axis=1, tiled=True))
    product_b = product.astype(jnp.bfloat16)
    left_part = jnp.einsum("sfi,sic->sfc", pick_left, product_b, preferred_element_type=jnp.float32)
    right_part = jnp.einsum(
        "sfi,sic->sfc", pick_right, product_b, preferred_element_type=jnp.float32
    )
    partial_faces = jnp.stack([left_part, right_part], axis=1)
    boundary = lax.psum(partial_faces.astype(jnp.bfloat16), ("crow", "ccol"))
    extended = padded(boundary, (("sub", 0),), 1)
    from_before = extended[:sub_count, 1]
    from_after = extended[2:, 0]
    added_left = jnp.einsum(
        "sfi,sfc->sic", pick_left, from_before, preferred_element_type=jnp.float32
    )
    added_right = jnp.einsum(
        "sfi,sfc->sic", pick_right, from_after, preferred_element_type=jnp.float32
    )
    return product_b.astype(jnp.float32) + added_left + added_right


def coarse_step(restricted, coarse_inverse, coarse_index):
    sub_count, mode_count, case_count = restricted.shape
    flat_rows = restricted.reshape(sub_count * mode_count, case_count)
    flat_index = coarse_index.reshape(-1)
    owned_rows, block_width = coarse_inverse.shape
    block_index = lax.axis_index(("crow", "ccol"))
    arrived, arrived_index = (
        lax.all_gather(flat_rows, "sub", axis=0, tiled=True),
        lax.all_gather(flat_index, "sub", axis=0, tiled=True),
    )
    shifted_place = arrived_index - block_index * block_width
    inside = (shifted_place >= 0) & (shifted_place < block_width)
    arrived_place = jnp.where(inside, shifted_place, block_width)
    ordered = (
        jnp.zeros((block_width + 1, case_count), jnp.bfloat16)
        .at[arrived_place]
        .set(arrived)[:block_width]
    )
    partial_coarse = jnp.dot(coarse_inverse, ordered, preferred_element_type=jnp.float32)
    coarse = lax.psum(partial_coarse, ("crow", "ccol")).astype(jnp.bfloat16)
    everything = lax.all_gather(coarse, "sub", axis=0, tiled=True)
    picked = everything[flat_index]
    return picked.reshape(sub_count, mode_count, case_count)


def precondition(local_part, residual_rows, coarse_basis, coarse_inverse, coarse_index):
    partial_modes = jnp.einsum(
        "sik,sic->skc", coarse_basis, residual_rows, preferred_element_type=jnp.float32
    )
    restricted = lax.psum(partial_modes, ("crow", "ccol")).astype(jnp.bfloat16)
    picked = coarse_step(restricted, coarse_inverse, coarse_index)
    return local_part + jnp.einsum(
        "sik,skc->sic", coarse_basis, picked, preferred_element_type=jnp.float32
    )


def body(
    loads,
    stiffness,
    local_inverse,
    coarse_basis,
    coarse_inverse,
    coarse_index,
    left_rows,
    right_rows,
):
    sub_count, row_count, iface_count = stiffness.shape
    group_index = lax.axis_index(("crow", "ccol"))
    first_row = group_index * row_count
    loads_rows = lax.dynamic_slice_in_dim(loads, first_row, row_count, 1)
    local_rows = first_row + jnp.arange(row_count, dtype=jnp.int32)
    pick_left = (left_rows[:, :, None] == local_rows[None, None, :]).astype(jnp.bfloat16)
    pick_right = (right_rows[:, :, None] == local_rows[None, None, :]).astype(jnp.bfloat16)
    first_local = jnp.einsum(
        "sij,sjc->sic", local_inverse, loads, preferred_element_type=jnp.float32
    )
    first_pass = precondition(first_local, loads_rows, coarse_basis, coarse_inverse, coarse_index)
    image_first = apply_stiffness(first_pass, stiffness, pick_left, pick_right)
    residual_b = (loads_rows.astype(jnp.float32) - image_first).astype(jnp.bfloat16)
    second_local = fold_product(
        local_inverse, lax.all_gather(residual_b, ("crow", "ccol"), axis=1, tiled=True)
    )
    second_pass = first_pass + precondition(
        second_local, residual_b, coarse_basis, coarse_inverse, coarse_index
    )
    image_second = apply_stiffness(second_pass, stiffness, pick_left, pick_right)
    final_residual = loads_rows.astype(jnp.float32) - image_second
    return (second_pass, final_residual)


def solution(mesh):
    return jax.shard_map(
        body,
        mesh=mesh,
        in_specs=(
            P("sub", None, None),
            P("sub", ("crow", "ccol"), None),
            P("sub", ("crow", "ccol"), None),
            P("sub", ("crow", "ccol"), None),
            P("sub", ("crow", "ccol")),
            P("sub", None),
            P("sub", None),
            P("sub", None),
        ),
        out_specs=(P("sub", ("crow", "ccol"), None), P("sub", ("crow", "ccol"), None)),
        check_vma=False,
    )
```

profile of v0, /device:TPU:6, one launch (start us, length us, event | category | flops | bytes accessed | tf_op | source)
XLA Modules:
  0.0 929.7 jit_solution(8455041256860478172)
XLA Ops:
  8.3 34.2 %psum.42 = bf16[2,48,128]{2,1,0:T(8,128)(2,1)} all-reduce(f32[2,48,128]{2,1,0:T(8,128)S(1)} %convolution_bitcast_fusion.4), channel_id=1, replica_groups=mesh['sub'=64,'crow'=4,'ccol'=2] {'crow','ccol'}, use_global_device_ids=true, to_apply=%region_0.0 | all-reduce | flops 12288 | bytes 73728 | tf_op jit(solution)/shard_map/psum | solution.py:77
  45.6 282.8 %all-reduce = s32[6144]{0:T(1024)S(1)} all-reduce(s32[6144]{0:T(1024)S(1)} %dynamic-update-slice), channel_id=1, replica_groups=mesh['sub'=64,'crow'=4,'ccol'=2] {'sub'}, use_global_device_ids=true, to_apply=%add | all-reduce | flops 6144 | bytes 49152
  328.4 16.2 %scatter_custom_fusion = bf16[769,128]{1,0:T(8,128)(2,1)S(1)} fusion(s32[6144]{0:T(1024)S(1)} %compare_select_fusion, bf16[6144,128]{1,0:T(8,128)(2,1)} %all-gather.5.cloned.1.call-done, bf16[]{:T(256)} %constant.10.clone.1), kind=kCustom, calls=%fused_computation.46 | custom fusion | bytes 197376 | tf_op jit(solution)/shard_map/scatter | solution.py:64
  345.7 30.7 %psum.43 = bf16[96,128]{1,0:T(8,128)(2,1)} all-reduce(f32[96,128]{1,0:T(8,128)S(1)} %convolution_bitcast_fusion.3), channel_id=1, replica_groups=mesh['sub'=64,'crow'=4,'ccol'=2] {'crow','ccol'}, use_global_device_ids=true, to_apply=%region_2.3 | all-reduce | flops 12288 | bytes 73728 | tf_op jit(solution)/shard_map/psum | solution.py:67
  377.2 75.1 %all-gather.7.cloned.1.call-done = bf16[6144,128]{1,0:T(8,128)(2,1)} async-done(((bf16[96,128]{1,0:T(8,128)(2,1)}), bf16[6144,128]{1,0:T(8,128)(2,1)}) %all-gather.7.cloned.1.call-update) | async-done | bytes 1572880 | tf_op jit(solution)/shard_map/all_gather | solution.py:68
  452.4 2.2 gather_fusion
  455.9 27.2 %all_gather.28 = bf16[2,1024,128]{2,1,0:T(8,128)(2,1)S(1)} all-gather(bf16[2,128,128]{2,1,0:T(8,128)(2,1)S(1)} %get-tuple-element.6), channel_id=1, replica_groups=mesh['sub'=64,'crow'=4,'ccol'=2] {'crow','ccol'}, dimensions={1}, use_global_device_ids=true | all-gather | bytes 589824 | tf_op jit(solution)/shard_map/all_gather | solution.py:28
  484.7 65.4 %all-reduce.4.cloned.1.call-done = bf16[2,2,128,128]{3,2,0,1:T(8,128)(2,1)} async-done(((bf16[2,2,128,128]{3,2,0,1:T(8,128)(2,1)}), bf16[2,2,128,128]{3,2,0,1:T(8,128)(2,1)}) %all-reduce.4.cloned.1.call-update) | async-done | bytes 131088 | tf_op jit(solution)/shard_map/psum | solution.py:35
  550.9 8.1 collective-permute-start.1
  559.1 1.9 collective-permute-start
  562.2 6.5 collective-permute-done
  569.8 30.8 %psum.45 = bf16[2,48,128]{2,1,0:T(8,128)(2,1)} all-reduce(f32[2,48,128]{2,1,0:T(8,128)S(1)} %convolution_bitcast_fusion.2), channel_id=1, replica_groups=mesh['sub'=64,'crow'=4,'ccol'=2] {'crow','ccol'}, use_global_device_ids=true, to_apply=%region_4.5 | all-reduce | flops 12288 | bytes 73728 | tf_op jit(solution)/shard_map/psum | solution.py:77
  600.7 77.5 %all-gather.9.cloned.1.call-done = bf16[6144,128]{1,0:T(8,128)(2,1)} async-done(((bf16[96,128]{1,0:T(8,128)(2,1)}), bf16[6144,128]{1,0:T(8,128)(2,1)}) %all-gather.9.cloned.1.call-update) | async-done | bytes 1572880 | tf_op jit(solution)/shard_map/all_gather | solution.py:55
  678.2 16.2 %scatter_custom_fusion.1 = bf16[769,128]{1,0:T(8,128)(2,1)S(1)} fusion(s32[6144]{0:T(1024)S(1)} %compare_select_fusion, bf16[6144,128]{1,0:T(8,128)(2,1)} %all-gather.9.cloned.1.call-done, bf16[]{:T(256)} %constant.10.clone.1), kind=kCustom, calls=%fused_computation.44 | custom fusion | bytes 197376 | tf_op jit(solution)/shard_map/scatter | solution.py:64
  694.6 30.9 %psum.46 = bf16[96,128]{1,0:T(8,128)(2,1)} all-reduce(f32[96,128]{1,0:T(8,128)S(1)} %convolution_bitcast_fusion.1), channel_id=1, replica_groups=mesh['sub'=64,'crow'=4,'ccol'=2] {'crow','ccol'}, use_global_device_ids=true, to_apply=%region_6.7 | all-reduce | flops 12288 | bytes 73728 | tf_op jit(solution)/shard_map/psum | solution.py:67
  725.6 27.3 %all_gather.29 = bf16[2,1024,128]{2,1,0:T(8,128)(2,1)S(1)} all-gather(bf16[2,128,128]{2,1,0:T(8,128)(2,1)S(1)} %fusion.6), channel_id=1, replica_groups=mesh['sub'=64,'crow'=4,'ccol'=2] {'crow','ccol'}, dimensions={1}, use_global_device_ids=true | all-gather | bytes 589824 | tf_op jit(solution)/shard_map/all_gather | solution.py:108
  752.8 52.2 %all-gather.11.cloned.1.call-done = bf16[6144,128]{1,0:T(8,128)(2,1)} async-done(((bf16[96,128]{1,0:T(8,128)(2,1)}), bf16[6144,128]{1,0:T(8,128)(2,1)}) %all-gather.11.cloned.1.call-update) | async-done | bytes 1572880 | tf_op jit(solution)/shard_map/all_gather | solution.py:68
  805.1 2.2 gather_fusion.1
  808.5 27.2 %all_gather.32 = bf16[2,1024,128]{2,1,0:T(8,128)(2,1)S(1)} all-gather(bf16[2,128,128]{2,1,0:T(8,128)(2,1)S(1)} %get-tuple-element.8), channel_id=1, replica_groups=mesh['sub'=64,'crow'=4,'ccol'=2] {'crow','ccol'}, dimensions={1}, use_global_device_ids=true | all-gather | bytes 589824 | tf_op jit(solution)/shard_map/all_gather | solution.py:28
  837.2 65.4 %all-reduce.6.cloned.1.call-done = bf16[2,2,128,128]{3,2,0,1:T(8,128)(2,1)} async-done(((bf16[2,2,128,128]{3,2,0,1:T(8,128)(2,1)}), bf16[2,2,128,128]{3,2,0,1:T(8,128)(2,1)}) %all-reduce.6.cloned.1.call-update) | async-done | bytes 131088 | tf_op jit(solution)/shard_map/psum | solution.py:35
  903.5 8.1 collective-permute-start.3
  911.6 1.9 collective-permute-start.2
  914.7 6.5 collective-permute-done.2
  921.2 1.6 fusion.3
  (59 shorter events, 16.5 us)
Async XLA Ops:
  7.2 448.4 %copy-start = (bf16[2,128,1024]{2,1,0:T(8,128)(2,1)S(1)}, bf16[2,128,1024]{2,1,0:T(8,128)(2,1)}, u32[]{:S(2)}) copy-start(bf16[2,128,1024]{2,1,0:T(8,128)(2,1)} %param.10) | copy-start | bytes 1572868
  7.2 448.4 %copy-start.2 = (bf16[2,1024,128]{2,1,0:T(8,128)(2,1)S(1)}, bf16[2,1024,128]{2,1,0:T(8,128)(2,1)}, u32[]{:S(2)}) copy-start(bf16[2,1024,128]{2,1,0:T(8,128)(2,1)} %param.8) | copy-start | bytes 1572868
  7.2 321.2 %all-gather.5.cloned.1.call-start = ((), (), s32[]{:S(2)}) async-start(), calls=%async_computation | async-start | bytes 1597440 | tf_op jit(solution)/shard_map/all_gather | solution.py:55
  42.5 409.8 %all-gather.7.cloned.1.call-start = ((), (), s32[]{:S(2)}) async-start(), calls=%async_computation.1 | async-start | bytes 1597440 | tf_op jit(solution)/shard_map/all_gather | solution.py:68
  328.3 154.7 %copy-start.1 = (bf16[2,128,1024]{2,1,0:T(8,128)(2,1)S(1)}, bf16[2,128,1024]{2,1,0:T(8,128)(2,1)}, u32[]{:S(2)}) copy-start(bf16[2,128,1024]{2,1,0:T(8,128)(2,1)} %param.9) | copy-start | bytes 1572868
  376.4 173.7 %all-reduce.4.cloned.1.call-start = ((), (), s32[]{:S(2)}) async-start(), calls=%async_computation.2 | async-start | bytes 262144 | tf_op jit(solution)/shard_map/psum | solution.py:35
  455.6 27.8 %copy-start.5 = (s32[2,128]{1,0:T(2,128)S(1)}, s32[2,128]{1,0:T(2,128)}, u32[]{:S(2)}) copy-start(s32[2,128]{1,0:T(2,128)} %param.15) | copy-start | bytes 3076
  455.6 28.1 %copy-start.6 = (s32[2,128]{1,0:T(2,128)S(1)}, s32[2,128]{1,0:T(2,128)}, u32[]{:S(2)}) copy-start(s32[2,128]{1,0:T(2,128)} %param.14) | copy-start | bytes 3076
  483.1 86.6 %copy-start.4 = (bf16[2,128,48]{1,2,0:T(8,128)(2,1)S(1)}, bf16[2,128,48]{1,2,0:T(8,128)(2,1)}, u32[]{:S(2)}) copy-start(bf16[2,128,48]{1,2,0:T(8,128)(2,1)} %param.11) | copy-start | bytes 73732
  483.1 211.3 %copy-start.3 = (bf16[96,768]{1,0:T(8,128)(2,1)S(1)}, bf16[96,768]{1,0:T(8,128)(2,1)}, u32[]{:S(2)}) copy-start(bf16[96,768]{1,0:T(8,128)(2,1)} %param.12) | copy-start | bytes 442372
  484.7 193.5 %all-gather.9.cloned.1.call-start = ((), (), s32[]{:S(2)}) async-start(), calls=%async_computation.3 | async-start | bytes 1597440 | tf_op jit(solution)/shard_map/all_gather | solution.py:55
  550.9 10.3 %collective-permute-start.1 = (bf16[1,2,128,128]{3,2,0,1:T(8,128)(2,1)S(1)}, bf16[1,2,128,128]{3,2,0,1:T(8,128)(2,1)S(1)}, u32[]{:S(2)}, u32[]{:S(2)}) collective-permute-start(bf16[1,2,128,128]{3,2,0,1:T(8,128)(2,1)S(1)} %get-tuple-element.5), channel_id=1, source_target_pairs={{8,0},{16,8},{24,16},{32,24},{40,32},{48,40},{56,48},{64,56},{72,6... | collective-permute-start | bytes 196616 | tf_op jit(solution)/shard_map/ppermute | solution.py:16
  559.1 9.6 %collective-permute-start = (bf16[1,2,128,128]{3,2,0,1:T(8,128)(2,1)S(1)}, bf16[1,2,128,128]{3,2,0,1:T(8,128)(2,1)S(1)}, u32[]{:S(2)}, u32[]{:S(2)}) collective-permute-start(bf16[1,2,128,128]{3,2,0,1:T(8,128)(2,1)S(1)} %get-tuple-element.4), channel_id=1, source_target_pairs={{0,8},{8,16},{16,24},{24,32},{32,40},{40,48},{48,56},{56,64},{64,7... | collective-permute-start | bytes 196616 | tf_op jit(solution)/shard_map/ppermute | solution.py:13
  600.6 204.4 %all-gather.11.cloned.1.call-start = ((), (), s32[]{:S(2)}) async-start(), calls=%async_computation.4 | async-start | bytes 1597440 | tf_op jit(solution)/shard_map/all_gather | solution.py:68
  725.5 177.1 %all-reduce.6.cloned.1.call-start = ((), (), s32[]{:S(2)}) async-start(), calls=%async_computation.5 | async-start | bytes 262144 | tf_op jit(solution)/shard_map/psum | solution.py:35
  903.5 10.3 %collective-permute-start.3 = (bf16[1,2,128,128]{3,2,0,1:T(8,128)(2,1)S(1)}, bf16[1,2,128,128]{3,2,0,1:T(8,128)(2,1)S(1)}, u32[]{:S(2)}, u32[]{:S(2)}) collective-permute-start(bf16[1,2,128,128]{3,2,0,1:T(8,128)(2,1)S(1)} %get-tuple-element.3), channel_id=1, source_target_pairs={{8,0},{16,8},{24,16},{32,24},{40,32},{48,40},{56,48},{64,56},{72,6... | collective-permute-start | bytes 196616 | tf_op jit(solution)/shard_map/ppermute | solution.py:16
  911.6 9.6 %collective-permute-start.2 = (bf16[1,2,128,128]{3,2,0,1:T(8,128)(2,1)S(1)}, bf16[1,2,128,128]{3,2,0,1:T(8,128)(2,1)S(1)}, u32[]{:S(2)}, u32[]{:S(2)}) collective-permute-start(bf16[1,2,128,128]{3,2,0,1:T(8,128)(2,1)S(1)} %get-tuple-element.2), channel_id=1, source_target_pairs={{0,8},{8,16},{16,24},{24,32},{32,40},{40,48},{48,56},{56,64},{64,7... | collective-permute-start | bytes 196616 | tf_op jit(solution)/shard_map/ppermute | solution.py:13
Sparse Core Ops, SparseCore 0:
  42.7 83.8 all-gather.4
  376.5 75.8 all-gather.6
  484.8 65.2 all-reduce.3
  600.8 77.3 all-gather.8
  725.6 79.3 all-gather.10
  837.3 65.2 all-reduce.5
where the time goes:
time: 931 us; the launch traced here: 930 us
  blocking collectives  491 us (53%)
  waiting for transfers between devices  349 us (37%)
  local copies, waits for them, and re-layouts  41.7 us (4%)
  starting transfers between devices  20.3 us (2%)
  between operations  15 us (2%)
  matrix products  11.1 us (1%)
    unnamed x1, blocking collectives  283 us
    psum x2, waiting for transfers between devices, apply_stiffness(): boundary = lax.psum(partial_faces.astype(jnp.bfloat16), ('crow', 'ccol'))  131 us
    all_gather x2, waiting for transfers between devices, coarse_step(): everything = lax.all_gather(coarse, 'sub', axis=0, tiled=True)  127 us
    all_gather x2, waiting for transfers between devices, coarse_step(): lax.all_gather(flat_rows, 'sub', axis=0, tiled=True)  77.5 us
    psum x2, blocking collectives, precondition(): restricted = lax.psum(partial_modes, ('crow', 'ccol')).astype(jnp.bfloat16)  65 us
    psum x2, blocking collectives, coarse_step(): coarse = lax.psum(partial_coarse, ('crow', 'ccol')).astype(jnp.bfloat16)  61.6 us
    all_gather x2, blocking collectives, apply_stiffness(): lax.all_gather(rounded, ('crow', 'ccol'), axis=1, tiled=True)  54.3 us
    scatter x2, local copies, waits for them, and re-layouts, coarse_step(): ordered = jnp.zeros((block_width + 1, case_count), jnp.bfloat16).at[arriv...  32.4 us
  transfers between devices with their start and end apart: 10, of which 9 were waited for; matrix products, arithmetic and copies ran while one was open for 1% of the time, Pallas kernels for 0%

commit v1 on v0

--- a/solution.py
+++ b/solution.py
@@ -32,7 +32,7 @@
         "sfi,sic->sfc", pick_right, product_b, preferred_element_type=jnp.float32
     )
     partial_faces = jnp.stack([left_part, right_part], axis=1)
-    boundary = lax.psum(partial_faces.astype(jnp.bfloat16), ("crow", "ccol"))
+    boundary = jnp.sum(lax.all_gather(partial_faces.astype(jnp.bfloat16), ("crow", "ccol")), axis=0)
     extended = padded(boundary, (("sub", 0),), 1)
     from_before = extended[:sub_count, 1]
     from_after = extended[2:, 0]

time: 931 us -> 879 us (0.944)
  waiting for transfers between devices: 349 us -> 298 us
    psum x2 -> x0, waiting for transfers between devices: 131 us -> none  [apply_stiffness(): boundary = lax.psum(partial_faces.astype(jnp.bfloat16), ('crow', 'ccol'))]
    all_gather x0 -> x2, waiting for transfers between devices: none -> 78.4 us  [apply_stiffness(): lax.all_gather(partial_faces.astype(jnp.bfloat16), ('crow', 'ccol'))]
  transfers between devices with their start and end apart: 10 -> 10, of which waited for: 9 -> 9; matrix products, arithmetic and copies ran while one was open for 1% -> 0% of each run, Pallas kernels for 0% -> 0%
where the time goes in v1:
time: 879 us; the launch traced here: 876 us
  blocking collectives  492 us (56%)
  waiting for transfers between devices  298 us (34%)
  local copies, waits for them, and re-layouts  41.3 us (5%)
  starting transfers between devices  19.2 us (2%)
  between operations  15 us (2%)
    unnamed x1, blocking collectives  283 us
    all_gather x2, waiting for transfers between devices, coarse_step(): everything = lax.all_gather(coarse, 'sub', axis=0, tiled=True)  127 us
    all_gather x2, waiting for transfers between devices, apply_stiffness(): lax.all_gather(partial_faces.astype(jnp.bfloat16), ('crow', 'ccol'))  78.4 us
    all_gather x2, waiting for transfers between devices, coarse_step(): lax.all_gather(flat_rows, 'sub', axis=0, tiled=True)  77 us
    psum x2, blocking collectives, precondition(): restricted = lax.psum(partial_modes, ('crow', 'ccol')).astype(jnp.bfloat16)  66.3 us
    psum x2, blocking collectives, coarse_step(): coarse = lax.psum(partial_coarse, ('crow', 'ccol')).astype(jnp.bfloat16)  61.6 us
    all_gather x2, blocking collectives, apply_stiffness(): lax.all_gather(rounded, ('crow', 'ccol'), axis=1, tiled=True)  54.3 us
    scatter x2, local copies, waits for them, and re-layouts, coarse_step(): ordered = jnp.zeros((block_width + 1, case_count), jnp.bfloat16).at[arriv...  32.4 us
  transfers between devices with their start and end apart: 10, of which 9 were waited for; matrix products, arithmetic and copies ran while one was open for 0% of the time, Pallas kernels for 0%

profile of v1, /device:TPU:6, one launch (start us, length us, event | category | flops | bytes accessed | tf_op | source)
XLA Modules:
  0.0 876.4 jit_solution(8212281979953833809)
XLA Ops:
  8.3 34.2 %psum.28 = bf16[2,48,128]{2,1,0:T(8,128)(2,1)} all-reduce(f32[2,48,128]{2,1,0:T(8,128)S(1)} %convolution_bitcast_fusion.4), channel_id=1, replica_groups=mesh['sub'=64,'crow'=4,'ccol'=2] {'crow','ccol'}, use_global_device_ids=true, to_apply=%region_0.0 | all-reduce | flops 12288 | bytes 73728 | tf_op jit(solution)/shard_map/psum | solution.py:77
  45.6 282.8 %all-reduce = s32[6144]{0:T(1024)S(1)} all-reduce(s32[6144]{0:T(1024)S(1)} %dynamic-update-slice), channel_id=1, replica_groups=mesh['sub'=64,'crow'=4,'ccol'=2] {'sub'}, use_global_device_ids=true, to_apply=%add | all-reduce | flops 6144 | bytes 49152
  328.4 16.2 %scatter_custom_fusion = bf16[769,128]{1,0:T(8,128)(2,1)S(1)} fusion(s32[6144]{0:T(1024)S(1)} %compare_select_fusion, bf16[6144,128]{1,0:T(8,128)(2,1)} %all-gather.7.cloned.1.call-done, bf16[]{:T(256)} %constant.10.clone.1), kind=kCustom, calls=%fused_computation.46 | custom fusion | bytes 197376 | tf_op jit(solution)/shard_map/scatter | solution.py:64
  345.7 30.7 %psum.29 = bf16[96,128]{1,0:T(8,128)(2,1)} all-reduce(f32[96,128]{1,0:T(8,128)S(1)} %convolution_bitcast_fusion.3), channel_id=1, replica_groups=mesh['sub'=64,'crow'=4,'ccol'=2] {'crow','ccol'}, use_global_device_ids=true, to_apply=%region_2.3 | all-reduce | flops 12288 | bytes 73728 | tf_op jit(solution)/shard_map/psum | solution.py:67
  377.2 75.1 %all-gather.9.cloned.1.call-done = bf16[6144,128]{1,0:T(8,128)(2,1)} async-done(((bf16[96,128]{1,0:T(8,128)(2,1)}), bf16[6144,128]{1,0:T(8,128)(2,1)}) %all-gather.9.cloned.1.call-update) | async-done | bytes 1572880 | tf_op jit(solution)/shard_map/all_gather | solution.py:68
  452.4 2.2 gather_fusion
  455.9 27.2 %all_gather.36 = bf16[2,1024,128]{2,1,0:T(8,128)(2,1)S(1)} all-gather(bf16[2,128,128]{2,1,0:T(8,128)(2,1)S(1)} %get-tuple-element.6), channel_id=1, replica_groups=mesh['sub'=64,'crow'=4,'ccol'=2] {'crow','ccol'}, dimensions={1}, use_global_device_ids=true | all-gather | bytes 589824 | tf_op jit(solution)/shard_map/all_gather | solution.py:28
  484.7 39.2 %all-gather.11.cloned.1.call-done = bf16[8,2,2,128,128]{4,3,2,1,0:T(8,128)(2,1)} async-done(((bf16[1,2,2,128,128]{4,3,2,1,0:T(8,128)(2,1)}), bf16[8,2,2,128,128]{4,3,2,1,0:T(8,128)(2,1)}) %all-gather.11.cloned.1.call-update) | async-done | bytes 1048592 | tf_op jit(solution)/shard_map/all_gather | solution.py:35
  525.3 7.6 collective-permute-start.1
  532.9 1.9 collective-permute-start
  535.2 7.2 collective-permute-done
  542.8 32.1 %psum.30 = bf16[2,48,128]{2,1,0:T(8,128)(2,1)} all-reduce(f32[2,48,128]{2,1,0:T(8,128)S(1)} %convolution_bitcast_fusion.2), channel_id=1, replica_groups=mesh['sub'=64,'crow'=4,'ccol'=2] {'crow','ccol'}, use_global_device_ids=true, to_apply=%region_4.5 | all-reduce | flops 12288 | bytes 73728 | tf_op jit(solution)/shard_map/psum | solution.py:77
  574.9 77.0 %all-gather.13.cloned.1.call-done = bf16[6144,128]{1,0:T(8,128)(2,1)} async-done(((bf16[96,128]{1,0:T(8,128)(2,1)}), bf16[6144,128]{1,0:T(8,128)(2,1)}) %all-gather.13.cloned.1.call-update) | async-done | bytes 1572880 | tf_op jit(solution)/shard_map/all_gather | solution.py:55
  651.9 16.2 %scatter_custom_fusion.1 = bf16[769,128]{1,0:T(8,128)(2,1)S(1)} fusion(s32[6144]{0:T(1024)S(1)} %compare_select_fusion, bf16[6144,128]{1,0:T(8,128)(2,1)} %all-gather.13.cloned.1.call-done, bf16[]{:T(256)} %constant.10.clone.1), kind=kCustom, calls=%fused_computation.44 | custom fusion | bytes 197376 | tf_op jit(solution)/shard_map/scatter | solution.py:64
  668.3 30.9 %psum.31 = bf16[96,128]{1,0:T(8,128)(2,1)} all-reduce(f32[96,128]{1,0:T(8,128)S(1)} %convolution_bitcast_fusion.1), channel_id=1, replica_groups=mesh['sub'=64,'crow'=4,'ccol'=2] {'crow','ccol'}, use_global_device_ids=true, to_apply=%region_6.7 | all-reduce | flops 12288 | bytes 73728 | tf_op jit(solution)/shard_map/psum | solution.py:67
  699.3 27.3 %all_gather.38 = bf16[2,1024,128]{2,1,0:T(8,128)(2,1)S(1)} all-gather(bf16[2,128,128]{2,1,0:T(8,128)(2,1)S(1)} %fusion.6), channel_id=1, replica_groups=mesh['sub'=64,'crow'=4,'ccol'=2] {'crow','ccol'}, dimensions={1}, use_global_device_ids=true | all-gather | bytes 589824 | tf_op jit(solution)/shard_map/all_gather | solution.py:108
  726.6 52.2 %all-gather.15.cloned.1.call-done = bf16[6144,128]{1,0:T(8,128)(2,1)} async-done(((bf16[96,128]{1,0:T(8,128)(2,1)}), bf16[6144,128]{1,0:T(8,128)(2,1)}) %all-gather.15.cloned.1.call-update) | async-done | bytes 1572880 | tf_op jit(solution)/shard_map/all_gather | solution.py:68
  778.8 2.2 gather_fusion.1
  782.2 27.2 %all_gather.41 = bf16[2,1024,128]{2,1,0:T(8,128)(2,1)S(1)} all-gather(bf16[2,128,128]{2,1,0:T(8,128)(2,1)S(1)} %get-tuple-element.8), channel_id=1, replica_groups=mesh['sub'=64,'crow'=4,'ccol'=2] {'crow','ccol'}, dimensions={1}, use_global_device_ids=true | all-gather | bytes 589824 | tf_op jit(solution)/shard_map/all_gather | solution.py:28
  811.0 39.2 %all-gather.17.cloned.1.call-done = bf16[8,2,2,128,128]{4,3,2,1,0:T(8,128)(2,1)} async-done(((bf16[1,2,2,128,128]{4,3,2,1,0:T(8,128)(2,1)}), bf16[8,2,2,128,128]{4,3,2,1,0:T(8,128)(2,1)}) %all-gather.17.cloned.1.call-update) | async-done | bytes 1048592 | tf_op jit(solution)/shard_map/all_gather | solution.py:35
  850.2 1.4 reduce_sum.25
  851.6 7.6 collective-permute-start.3
  859.2 1.9 collective-permute-start.2
  861.4 7.2 collective-permute-done.2
  (63 shorter events, 14.6 us)
Async XLA Ops:
  7.2 448.4 %copy-start = (bf16[2,128,1024]{2,1,0:T(8,128)(2,1)S(1)}, bf16[2,128,1024]{2,1,0:T(8,128)(2,1)}, u32[]{:S(2)}) copy-start(bf16[2,128,1024]{2,1,0:T(8,128)(2,1)} %param.10) | copy-start | bytes 1572868
  7.2 448.4 %copy-start.2 = (bf16[2,1024,128]{2,1,0:T(8,128)(2,1)S(1)}, bf16[2,1024,128]{2,1,0:T(8,128)(2,1)}, u32[]{:S(2)}) copy-start(bf16[2,1024,128]{2,1,0:T(8,128)(2,1)} %param.8) | copy-start | bytes 1572868
  7.2 321.2 %all-gather.7.cloned.1.call-start = ((), (), s32[]{:S(2)}) async-start(), calls=%async_computation | async-start | bytes 1597440 | tf_op jit(solution)/shard_map/all_gather | solution.py:55
  42.5 409.8 %all-gather.9.cloned.1.call-start = ((), (), s32[]{:S(2)}) async-start(), calls=%async_computation.1 | async-start | bytes 1597440 | tf_op jit(solution)/shard_map/all_gather | solution.py:68
  328.3 154.7 %copy-start.1 = (bf16[2,128,1024]{2,1,0:T(8,128)(2,1)S(1)}, bf16[2,128,1024]{2,1,0:T(8,128)(2,1)}, u32[]{:S(2)}) copy-start(bf16[2,128,1024]{2,1,0:T(8,128)(2,1)} %param.9) | copy-start | bytes 1572868
  376.4 147.5 %all-gather.11.cloned.1.call-start = ((), (), s32[]{:S(2)}) async-start(), calls=%async_computation.2 | async-start | bytes 1179648 | tf_op jit(solution)/shard_map/all_gather | solution.py:35
  455.6 27.8 %copy-start.5 = (s32[2,128]{1,0:T(2,128)S(1)}, s32[2,128]{1,0:T(2,128)}, u32[]{:S(2)}) copy-start(s32[2,128]{1,0:T(2,128)} %param.15) | copy-start | bytes 3076
  455.6 28.1 %copy-start.6 = (s32[2,128]{1,0:T(2,128)S(1)}, s32[2,128]{1,0:T(2,128)}, u32[]{:S(2)}) copy-start(s32[2,128]{1,0:T(2,128)} %param.14) | copy-start | bytes 3076
  483.4 59.3 %copy-start.4 = (bf16[2,128,48]{1,2,0:T(8,128)(2,1)S(1)}, bf16[2,128,48]{1,2,0:T(8,128)(2,1)}, u32[]{:S(2)}) copy-start(bf16[2,128,48]{1,2,0:T(8,128)(2,1)} %param.11) | copy-start | bytes 73732
  484.0 184.1 %copy-start.3 = (bf16[96,768]{1,0:T(8,128)(2,1)S(1)}, bf16[96,768]{1,0:T(8,128)(2,1)}, u32[]{:S(2)}) copy-start(bf16[96,768]{1,0:T(8,128)(2,1)} %param.12) | copy-start | bytes 442372
  484.7 167.2 %all-gather.13.cloned.1.call-start = ((), (), s32[]{:S(2)}) async-start(), calls=%async_computation.3 | async-start | bytes 1597440 | tf_op jit(solution)/shard_map/all_gather | solution.py:55
  525.3 9.6 %collective-permute-start.1 = (bf16[1,2,128,128]{3,2,0,1:T(8,128)(2,1)S(1)}, bf16[1,2,128,128]{3,2,0,1:T(8,128)(2,1)S(1)}, u32[]{:S(2)}, u32[]{:S(2)}) collective-permute-start(bf16[1,2,128,128]{3,2,0,1:T(8,128)(2,1)S(1)} %get-tuple-element.5), channel_id=1, source_target_pairs={{8,0},{16,8},{24,16},{32,24},{40,32},{48,40},{56,48},{64,56},{72,6... | collective-permute-start | bytes 196616 | tf_op jit(solution)/shard_map/ppermute | solution.py:16
  532.9 9.5 %collective-permute-start = (bf16[1,2,128,128]{3,2,0,1:T(8,128)(2,1)S(1)}, bf16[1,2,128,128]{3,2,0,1:T(8,128)(2,1)S(1)}, u32[]{:S(2)}, u32[]{:S(2)}) collective-permute-start(bf16[1,2,128,128]{3,2,0,1:T(8,128)(2,1)S(1)} %get-tuple-element.4), channel_id=1, source_target_pairs={{0,8},{8,16},{16,24},{24,32},{32,40},{40,48},{48,56},{56,64},{64,7... | collective-permute-start | bytes 196616 | tf_op jit(solution)/shard_map/ppermute | solution.py:13
  574.9 203.9 %all-gather.15.cloned.1.call-start = ((), (), s32[]{:S(2)}) async-start(), calls=%async_computation.4 | async-start | bytes 1597440 | tf_op jit(solution)/shard_map/all_gather | solution.py:68
  699.2 151.0 %all-gather.17.cloned.1.call-start = ((), (), s32[]{:S(2)}) async-start(), calls=%async_computation.5 | async-start | bytes 1179648 | tf_op jit(solution)/shard_map/all_gather | solution.py:35
  851.6 9.6 %collective-permute-start.3 = (bf16[1,2,128,128]{3,2,0,1:T(8,128)(2,1)S(1)}, bf16[1,2,128,128]{3,2,0,1:T(8,128)(2,1)S(1)}, u32[]{:S(2)}, u32[]{:S(2)}) collective-permute-start(bf16[1,2,128,128]{3,2,0,1:T(8,128)(2,1)S(1)} %get-tuple-element.3), channel_id=1, source_target_pairs={{8,0},{16,8},{24,16},{32,24},{40,32},{48,40},{56,48},{64,56},{72,6... | collective-permute-start | bytes 196616 | tf_op jit(solution)/shard_map/ppermute | solution.py:16
  859.2 9.5 %collective-permute-start.2 = (bf16[1,2,128,128]{3,2,0,1:T(8,128)(2,1)S(1)}, bf16[1,2,128,128]{3,2,0,1:T(8,128)(2,1)S(1)}, u32[]{:S(2)}, u32[]{:S(2)}) collective-permute-start(bf16[1,2,128,128]{3,2,0,1:T(8,128)(2,1)S(1)} %get-tuple-element.2), channel_id=1, source_target_pairs={{0,8},{8,16},{16,24},{24,32},{32,40},{40,48},{48,56},{56,64},{64,7... | collective-permute-start | bytes 196616 | tf_op jit(solution)/shard_map/ppermute | solution.py:13
Sparse Core Ops, SparseCore 0:
  42.7 83.8 all-gather.6
  376.5 75.8 all-gather.8
  484.8 39.0 all-gather.10
  575.0 76.8 all-gather.12
  699.3 79.3 all-gather.14
  811.1 39.0 all-gather.16
